TPU v7x, 32 devices: a whole 2x2x4 slice. The times are simulated.
32 devices in a mesh: dp: 4 (over x, core), fsdp: 8 (over z, y).
Axes of the slice: x: 2, y: 2, z: 4, core: 2. Of those that a mesh axis runs over, the one named last changes fastest.
Arguments:
- token_ids: int32 [4096], P('dp'), may hold values from 0 to 15263, as said below
- embed_table: bfloat16 [15264, 768], P('fsdp'), may hold values from -16 to 16, as said below
- w_qkv: bfloat16 [768, 2304], P('fsdp'), may hold values from -2 to 2
- w_out: bfloat16 [768, 768], P('fsdp'), may hold values from -0.21875 to 0.21875
- ln_gain: float32 [768], replicated, may hold values from 0.5 to 1.5
- ln_bias: float32 [768], replicated, may hold values from -1 to 1
- centroids_t: bfloat16 [768, 32768], P('fsdp', 'dp'), may hold values from -24 to 24
- assignments: int32 [4096], replicated, may hold values from 0 to 32767, as said below
Outputs:
- token_loss: float32 [4096], P(('dp', 'fsdp'))
- new_centroids: float32 [32768, 768], P(('dp', 'fsdp'))
Inputs may be any that keep to these rules, and one draw needn't show every extreme that they name: `token_ids`: id 0 is padding; a passage may end in a run of padding. `embed_table`: token embeddings of order one. `assignments`: cluster sizes are skewed.
All inputs are finite; a program needn't handle non-finite values.
Results may differ from a plain program's by a relative error of at most 0.0055.
Values may be sent and summed in bfloat16 or wider, within the bound.
A program may use at most 64 MiB of HBM per device.

v0:
```python
import functools
import math

import jax
import jax.numpy as jnp
from jax import lax
from jax.experimental import pallas as pl
from jax.experimental.pallas import tpu as pltpu
from jax.sharding import PartitionSpec as P

HEADS = 12
HEAD = 64
SEQ = 128


def joined(shard, axis, combine):
    everything = jax.tree.map(lambda part: lax.all_gather(part, axis), shard)
    initial = jax.tree.map(lambda part: part[0], everything)

    def lap(k, so_far):
        return combine(so_far, jax.tree.map(lambda part: part[k], everything))

    return lax.fori_loop(1, lax.axis_size(axis), lap, initial)


def layer_norm(values, ln_gain, ln_bias):
    center = values - jnp.mean(values, axis=-1, keepdims=True)
    spread = jnp.mean(center * center, axis=-1, keepdims=True)
    return center * lax.rsqrt(spread + 1e-05) * ln_gain + ln_bias


def encode(inputs, qkv_full, out_full, ln_gain, ln_bias):
    passages = inputs.shape[0] // SEQ
    packed = jnp.dot(inputs, qkv_full, preferred_element_type=jnp.float32).astype(jnp.bfloat16)
    packed = packed.reshape(passages, SEQ, 3, HEADS, HEAD)
    scores = jnp.einsum(
        "bqhd,bkhd->bhqk", packed[:, :, 0], packed[:, :, 1], preferred_element_type=jnp.float32
    ) * (1.0 / math.sqrt(HEAD))
    probs = jax.nn.softmax(scores, axis=-1).astype(jnp.bfloat16)
    context = jnp.einsum(
        "bhqk,bkhd->bqhd", probs, packed[:, :, 2], preferred_element_type=jnp.float32
    )
    context = context.astype(jnp.bfloat16).reshape(inputs.shape[0], HEADS * HEAD)
    mixed = jnp.dot(context, out_full, preferred_element_type=jnp.float32) + inputs.astype(
        jnp.float32
    )
    return layer_norm(mixed, ln_gain, ln_bias).astype(jnp.bfloat16)


def one_hot_sums(rows, targets, width):
    count = rows.shape[0]
    step_rows = math.gcd(count, 512)
    columns = jnp.arange(width, dtype=jnp.int32)

    def one_visit(totals, pieces):
        block_rows, block_targets = pieces
        hits = (block_targets[:, None] == columns[None, :]).astype(jnp.bfloat16)
        return (
            totals
            + lax.dot_general(
                hits, block_rows, (((0,), (0,)), ((), ())), preferred_element_type=jnp.float32
            ),
            None,
        )

    start = jnp.zeros((width, rows.shape[1]), jnp.float32)
    totals, unused = lax.scan(
        one_visit,
        start,
        (
            rows.reshape(count // step_rows, step_rows, rows.shape[1]),
            targets.reshape(count // step_rows, step_rows),
        ),
    )
    return totals


def combine_parts(first, second):
    peak = jnp.maximum(first[0], second[0])
    mass = first[1] * jnp.exp(first[0] - peak) + second[1] * jnp.exp(second[0] - peak)
    return (peak, mass, first[2] + second[2])


def shards(token_ids, embed_table, w_qkv, w_out, ln_gain, ln_bias, centroids_t, assignments):
    dp_size = lax.axis_size("dp")
    fsdp_size = lax.axis_size("fsdp")
    dp_rank = lax.axis_index("dp")
    fsdp_rank = lax.axis_index("fsdp")
    vocab_rows = embed_table.shape[0]
    local_ids = token_ids - fsdp_rank * vocab_rows
    inside = (local_ids >= 0) & (local_ids < vocab_rows)
    looked = jnp.take(embed_table, jnp.clip(local_ids, 0, vocab_rows - 1), axis=0)
    looked = jnp.where(inside[:, None], looked, jnp.zeros_like(looked))
    inputs = (
        lax.psum_scatter(looked, "fsdp", scatter_dimension=0, tiled=True)
        .astype(jnp.float32)
        .astype(jnp.bfloat16)
    )
    qkv_full, out_full, cent_full = (
        lax.all_gather(w_qkv, "fsdp", axis=0, tiled=True),
        lax.all_gather(w_out, "fsdp", axis=0, tiled=True),
        lax.all_gather(centroids_t, "fsdp", axis=0, tiled=True),
    )
    encoded = encode(inputs, qkv_full, out_full, ln_gain, ln_bias)
    own_rows = encoded.shape[0]
    width = encoded.shape[1]
    block_width = cent_full.shape[1]
    per_dev = block_width // fsdp_size
    slab = lax.all_gather(encoded, "dp", axis=0, tiled=True)
    slab_assign = lax.dynamic_index_in_dim(
        assignments.reshape(dp_size, fsdp_size, own_rows), fsdp_rank, 1, keepdims=False
    ).reshape(-1)
    owned = slab_assign - dp_rank * block_width
    slab_rows = slab.shape[0]
    step_rows = math.gcd(slab_rows, 512)
    columns = jnp.arange(block_width, dtype=jnp.int32)

    def body_visit(totals, pieces):
        block_rows, local = pieces
        logits = jnp.dot(block_rows, cent_full, preferred_element_type=jnp.float32)
        peak = jnp.max(logits, axis=1)
        mass = jnp.sum(jnp.exp(logits - peak[:, None]), axis=1)
        hits = local[:, None] == columns[None, :]
        picked = jnp.sum(jnp.where(hits, logits, 0.0), axis=1)
        return (totals, (peak, mass, picked))

    start = jnp.zeros((1,), jnp.float32)
    partial_value, stats = lax.scan(
        body_visit,
        start,
        (
            slab.reshape(slab_rows // step_rows, step_rows, width),
            owned.reshape(slab_rows // step_rows, step_rows),
        ),
    )
    peaks, masses, picks = (stats[0].reshape(-1), stats[1].reshape(-1), stats[2].reshape(-1))
    peaks, masses, picks = joined((peaks, masses, picks), "dp", combine_parts)
    peak_own = lax.dynamic_slice_in_dim(peaks, dp_rank * own_rows, own_rows)
    mass_own = lax.dynamic_slice_in_dim(masses, dp_rank * own_rows, own_rows)
    pick_own = lax.dynamic_slice_in_dim(picks, dp_rank * own_rows, own_rows)
    token_loss = jnp.log(mass_own) + peak_own - pick_own
    share = lax.all_to_all(encoded, "fsdp", split_axis=1, concat_axis=0, tiled=True)
    every_rows = lax.all_gather(share, "dp", axis=0, tiled=True)
    block_local = assignments - dp_rank * block_width
    partial_share = one_hot_sums(every_rows, block_local, block_width)
    totals = lax.all_to_all(partial_share, "fsdp", split_axis=0, concat_axis=1, tiled=True)
    base = dp_rank * block_width + fsdp_rank * per_dev
    targets = base + jnp.arange(per_dev, dtype=jnp.int32)
    counts = jnp.sum((assignments[:, None] == targets[None, :]).astype(jnp.int32), axis=0)
    previous = lax.dynamic_slice_in_dim(cent_full, fsdp_rank * per_dev, per_dev, 1).T.astype(
        jnp.float32
    )
    new_centroids = jnp.where(
        counts[:, None] > 0, totals / jnp.maximum(counts, 1)[:, None].astype(jnp.float32), previous
    )
    return (token_loss, new_centroids)


VMEM_LIMIT = 60 * 1024 * 1024
WHOLE_VMEM = pl.BlockSpec(memory_space=pltpu.VMEM)


class Place:
    def __init__(self, deep):
        self.deep = deep
        self.dp, self.fsdp = lax.axis_index("dp"), lax.axis_index("fsdp")
        self.x, self.c = self.dp // 2, self.dp % 2
        self.z, self.y = self.fsdp // 2, self.fsdp % 2

    def at(self, x=None, c=None, z=None, y=None):
        x, c = self.x if x is None else x, self.c if c is None else c
        z, y = self.z if z is None else z, self.y if y is None else y
        return {"dp": x * 2 + c, "fsdp": z * 2 + y}

    def greet(self):
        barrier = pltpu.get_barrier_semaphore()
        everyone = 8 * self.deep
        me = self.dp * 2 * self.deep + self.fsdp

        @pl.loop(1, everyone)
        def each(k):
            peer = (me + k) % everyone
            there = {"dp": peer // (2 * self.deep), "fsdp": peer % (2 * self.deep)}
            pl.semaphore_signal(barrier, inc=1, device_id=there, device_id_type=pl.DeviceIdType.MESH)

        pl.semaphore_wait(barrier, everyone - 1)


class Sender:
    def __init__(self, sems):
        self.sems, self.used, self.sent = sems, 0, []

    def send(self, src, dst, recv_sem, peer, when=None):
        copy = pltpu.make_async_remote_copy(
            src_ref=src,
            dst_ref=dst,
            send_sem=self.sems.at[self.used],
            recv_sem=recv_sem,
            device_id=peer,
            device_id_type=pl.DeviceIdType.MESH,
        )
        self.used += 1
        self.sent.append((copy, when))
        guarded(when, copy.start)

    def arrived(self, dst, recv_sem, peer, when=None):
        copy = pltpu.make_async_remote_copy(
            src_ref=dst,
            dst_ref=dst,
            send_sem=self.sems.at[0],
            recv_sem=recv_sem,
            device_id=peer,
            device_id_type=pl.DeviceIdType.MESH,
        )
        guarded(when, copy.wait_recv)

    def drain(self):
        for copy, when in self.sent:
            guarded(when, copy.wait_send)


def guarded(when, action):
    if when is None:
        action()
    else:
        pl.when(when)(action)


def near_first(z, k, deep):
    below, above = z, deep - 1 - z
    both = jnp.minimum(below, above)
    swing = z - (k + 1) // 2 if k % 2 else z + k // 2
    far = jnp.where(above > below, z + k - both, z - k + both)
    return jnp.where(k <= 2 * both, swing, far)


def passage(x, quarters, gain, bias, w_ref):
    width = x.shape[1]

    def dense(rows, q):
        weights = w_ref[q].reshape(width, width)
        return jnp.dot(rows, weights, preferred_element_type=jnp.float32)

    query, key, value = (dense(x, q).astype(jnp.bfloat16) for q in quarters[:3])
    context = []
    for head in range(HEADS):
        at = slice(head * HEAD, (head + 1) * HEAD)
        scores = lax.dot_general(
            query[:, at], key[:, at], (((1,), (1,)), ((), ())), preferred_element_type=jnp.float32
        ) * (1.0 / math.sqrt(HEAD))
        weight = jnp.exp(scores - jnp.max(scores, axis=1, keepdims=True))
        probs = (weight / jnp.sum(weight, axis=1, keepdims=True)).astype(jnp.bfloat16)
        context.append(jnp.dot(probs, value[:, at], preferred_element_type=jnp.float32))
    context = jnp.concatenate(context, axis=1).astype(jnp.bfloat16)
    mixed = dense(context, quarters[3]) + x.astype(jnp.float32)
    return layer_norm(mixed, gain, bias).astype(jnp.bfloat16)


def step_kernel(
    deep,
    ids_ref,
    table_ref,
    qkv_ref,
    out_w_ref,
    norm_ref,
    cent_ref,
    assign_ref,
    loss_ref,
    new_ref,
    rows,
    w,
    from_y,
    joined_y,
    from_z,
    cent,
    old,
    mine,
    tokens,
    counts,
    stat,
    got,
    load_sems,
    send_sems,
    y_sems,
    z_sems,
    w_sems,
    cent_sems,
    token_sems,
    stat_send,
    stat_recv,
):
    place = Place(deep)
    x, c, z, y = place.x, place.c, place.z, place.y
    own = place.fsdp
    parts = 2 * deep
    vocab_rows, width = table_ref.shape
    own_rows = mine.shape[0]
    per_dev = new_ref.shape[0]
    blocks = 4 * parts
    own_block = place.dp * parts + own
    quarter, across = x * 2 + c, (1 - x) * 2 + c
    partner, x_side, y_side = place.at(c=1 - c), place.at(x=1 - x), place.at(y=1 - y)
    up, down = place.at(z=jnp.minimum(z + 1, deep - 1)), place.at(z=jnp.maximum(z - 1, 0))

    loads = []
    for q in range(4):
        part = qkv_ref.at[:, pl.ds(q * width, width)] if q < 3 else out_w_ref
        loads.append(pltpu.make_async_copy(part, w.at[q, own], load_sems.at[q]))
    loads.append(
        pltpu.make_async_copy(
            cent_ref.at[:, pl.ds(pl.multiple_of(own * per_dev, 128), per_dev)], cent.at[own], load_sems.at[4]
        )
    )
    for load in loads:
        load.start()

    def look(y0):
        local = ids_ref[y0] - own * vocab_rows
        hot = local == lax.broadcasted_iota(jnp.int32, (deep * own_rows, vocab_rows), 1)
        found = jnp.dot(
            jnp.where(hot, 1.0, 0.0).astype(jnp.bfloat16), table_ref[...], preferred_element_type=jnp.float32
        )
        rows[y0] = found.astype(jnp.bfloat16).reshape(deep, own_rows, width)

    place.greet()
    out = Sender(send_sems)
    for load in loads:
        load.wait()

    home = w.at[quarter, own]
    out.send(home, home, w_sems.at[quarter, own], up, z + 1 < deep)
    out.send(home, home, w_sems.at[quarter, own], down, z > 0)
    for k in range(1, deep + 1):
        to = (z + k) % deep
        if k == 1:
            look(1 - y)
        out.send(rows.at[1 - y, to], from_y.at[to], y_sems.at[to], y_side)
    look(y)

    def spread(s):
        block = w.at[quarter, s]
        out.send(block, block, w_sems.at[quarter, s], x_side)
        out.send(block, block, w_sems.at[quarter, s], partner)

    def join(k):
        to = (z + k) % deep
        out.arrived(from_y.at[to], y_sems.at[to], y_side)
        joined_y[to] = from_y[to] + rows[y, to]
        if k < deep:
            out.send(joined_y.at[to], from_z.at[deep - k], z_sems.at[deep - k], place.at(z=to))

    for k in range(1, deep):
        z0 = near_first(z, k, deep)
        s = z0 * 2 + y
        block = w.at[quarter, s]
        out.arrived(block, w_sems.at[quarter, s], y_side)
        out.send(block, block, w_sems.at[quarter, s], up, (z0 < z) & (z + 1 < deep))
        out.send(block, block, w_sems.at[quarter, s], down, (z0 > z) & (z > 0))
        spread(s)
    for k in range(1, deep + 1):
        join(k)
    for k in range(deep):
        block = w.at[quarter, near_first(z, k, deep) * 2 + y]
        out.send(block, block, w_sems.at[quarter, near_first(z, k, deep) * 2 + y], y_side)

    def give(z0, y0):
        to = z0 * 2 + y0
        columns = pl.ds(pl.multiple_of(to * per_dev, 128), per_dev)
        out.send(
            cent_ref.at[:, columns], cent.at[own], cent_sems.at[own], {"dp": place.dp, "fsdp": to}
        )

    for k in range(1, deep):
        give((z + k) % deep, y)
    for k in range(deep):
        s = near_first(z, k, deep) * 2 + (1 - y)
        out.arrived(w.at[quarter, s], w_sems.at[quarter, s], y_side)
        spread(s)
    for k in range(deep):
        give((z + k) % deep, 1 - y)
    others = [near_first(z, k, deep) * 2 + y for k in range(1, deep)]
    others += [near_first(z, k, deep) * 2 + (1 - y) for k in range(deep)]
    for s in others:
        block = w.at[across, s]
        out.arrived(block, w_sems.at[across, s], x_side)
        out.send(block, block, w_sems.at[across, s], partner)
    total = joined_y[z]
    for k in range(1, deep):
        out.arrived(from_z.at[k], z_sems.at[k], y_side)
        total = total + from_z[k]
    for q in (x * 2 + (1 - c), (1 - x) * 2 + (1 - c)):
        for s in others:
            out.arrived(w.at[q, s], w_sems.at[q, s], partner)
    for first in range(0, own_rows, SEQ):
        mine[pl.ds(first, SEQ), :] = passage(
            total[first : first + SEQ], range(4), norm_ref[0:1, :], norm_ref[1:2, :], w
        )

    x_first = c == 1
    second_xy = (jnp.where(x_first, 1 - x, x), jnp.where(x_first, y, 1 - y))
    third_xy = (jnp.where(x_first, x, 1 - x), jnp.where(x_first, 1 - y, y))
    second = place.at(x=second_xy[0], y=second_xy[1])
    third = place.at(x=third_xy[0], y=third_xy[1])

    def number(x0, c0, z0, y0):
        return ((x0 * 2 + c0) * deep + z0) * 2 + y0

    def push(b, peer, when=None, src=None):
        block = tokens.at[b]
        out.send(block if src is None else src, block, token_sems.at[b], peer, when)

    def wait(b):
        out.arrived(tokens.at[b], token_sems.at[b], partner)

    push(own_block, up, z + 1 < deep, mine)
    push(own_block, down, z > 0, mine)
    for peer in (second, third, partner):
        push(own_block, peer, None, mine)
    tokens[own_block] = mine[...]
    new_ref[...] = jnp.zeros_like(new_ref)
    counts[...] = jnp.zeros_like(counts)
    base = own_block * per_dev
    centroid = lax.broadcasted_iota(jnp.int32, (per_dev, 2 * own_rows), 0) + base

    def pair_of(p):
        hits = centroid == assign_ref[p]
        return hits, tokens[pl.ds(p * 2, 2)].reshape(2 * own_rows, width)

    def add_up(p):
        hits, some = pair_of(p)
        ones = jnp.where(hits, 1.0, 0.0)
        counts[...] += jnp.sum(ones, axis=1, keepdims=True)
        new_ref[...] += jnp.dot(
            ones.astype(jnp.bfloat16), some, preferred_element_type=jnp.float32
        )

    def score(p):
        hits, some = pair_of(p)
        logits = lax.dot_general(
            old[...], some, (((1,), (1,)), ((), ())), preferred_element_type=jnp.float32
        )
        peak = jnp.max(logits, axis=0, keepdims=True)
        mass = jnp.sum(jnp.exp(logits - peak), axis=0, keepdims=True)
        pick = jnp.sum(jnp.where(hits, logits, 0.0), axis=0, keepdims=True)
        for half in range(2):
            b = p * 2 + half
            at = slice(half * own_rows, (half + 1) * own_rows)
            for k, row in enumerate((peak, mass, pick)):
                stat[b, pl.ds(k, 1), :] = row[:, at]
            pl.when(b != own_block)(stat_copy(b).start)

    def stat_copy(b):
        return pltpu.make_async_remote_copy(
            src_ref=stat.at[b],
            dst_ref=got.at[own_block],
            send_sem=stat_send.at[b],
            recv_sem=stat_recv.at[own_block],
            device_id={"dp": b // parts, "fsdp": b % parts},
            device_id_type=pl.DeviceIdType.MESH,
        )

    def take_centroids():
        for k in range(1, parts):
            s = (own + k) % parts
            out.arrived(cent.at[s], cent_sems.at[s], partner)
        old[...] = cent[...].reshape(width, per_dev).T

    def finish_line(z1):
        for xx, yy in (third_xy, (1 - x, 1 - y)):
            b = number(xx, c, z1, yy)
            wait(b)
            push(b, partner)

    def sums_of(z1, with_scores):
        for x0 in range(2):
            for y0 in range(2):
                wait(number(x0, 1 - c, z1, y0))

        @pl.loop(0, 4)
        def each(i):
            add_up(i * deep + z1)
            if with_scores:
                score(i * deep + z1)

    for k in range(deep):
        z0 = near_first(z, k, deep)
        if k > 0:
            b = number(x, c, z0, y)
            wait(b)
            push(b, up, (z0 < z) & (z + 1 < deep))
            push(b, down, (z0 > z) & (z > 0))
            push(b, second)
            push(b, third)
            push(b, partner)
        b = number(second_xy[0], c, z0, second_xy[1])
        wait(b)
        push(b, third)
        push(b, partner)
        if k >= 1:
            finish_line(near_first(z, k - 1, deep))
        if k == deep - 2:
            take_centroids()
        if k >= 2:
            sums_of(near_first(z, k - 2, deep), True)
    finish_line(near_first(z, deep - 1, deep))
    for k in range(deep - 2, deep):
        sums_of(near_first(z, k, deep), True)

    many = counts[...]
    new_ref[...] = jnp.where(
        many > 0, new_ref[...] / jnp.maximum(many, 1.0), old[...].astype(jnp.float32)
    )
    got[own_block] = stat[own_block]

    @pl.loop(0, blocks)
    def each_device(b):
        @pl.when(b != own_block)
        def done():
            stat_copy(b).wait_send()
            pltpu.make_async_remote_copy(
                src_ref=got.at[b],
                dst_ref=got.at[b],
                send_sem=stat_send.at[b],
                recv_sem=stat_recv.at[b],
                device_id=partner,
                device_id_type=pl.DeviceIdType.MESH,
            ).wait_recv()

    peaks, masses, picks = (got[:, k, :] for k in range(3))
    top = jnp.max(peaks, axis=0, keepdims=True)
    mass = jnp.sum(masses * jnp.exp(peaks - top), axis=0, keepdims=True)
    loss_ref[...] = jnp.log(mass) + top - jnp.sum(picks, axis=0, keepdims=True)
    out.drain()


def token_shards(token_ids, embed_table, w_qkv, w_out, ln_gain, ln_bias, centroids_t, assignments):
    parts = lax.axis_size("fsdp")
    deep = parts // 2
    blocks = 4 * parts
    width = embed_table.shape[1]
    feats = w_qkv.shape[0]
    own_rows = token_ids.shape[0] // parts
    per_dev = centroids_t.shape[1] // parts
    half = jnp.bfloat16
    block = (own_rows, width)
    sems = pltpu.SemaphoreType.DMA
    loss, new = pl.pallas_call(
        functools.partial(step_kernel, deep),
        out_shape=(
            jax.ShapeDtypeStruct((1, own_rows), jnp.float32),
            jax.ShapeDtypeStruct((per_dev, width), jnp.float32),
        ),
        in_specs=[
            WHOLE_VMEM,
            WHOLE_VMEM,
            WHOLE_VMEM,
            WHOLE_VMEM,
            WHOLE_VMEM,
            pl.BlockSpec(memory_space=pl.ANY),
            WHOLE_VMEM,
        ],
        out_specs=(WHOLE_VMEM, WHOLE_VMEM),
        scratch_shapes=[
            pltpu.VMEM((2, deep, *block), half),
            pltpu.VMEM((4, parts, feats, width), half),
            pltpu.VMEM((deep, *block), half),
            pltpu.VMEM((deep, *block), half),
            pltpu.VMEM((deep, *block), half),
            pltpu.VMEM((parts, feats, per_dev), half),
            pltpu.VMEM((per_dev, width), half),
            pltpu.VMEM(block, half),
            pltpu.VMEM((blocks, *block), half),
            pltpu.VMEM((per_dev, 1), jnp.float32),
            pltpu.VMEM((blocks, 8, own_rows), jnp.float32),
            pltpu.VMEM((blocks, 8, own_rows), jnp.float32),
            sems((5,)),
            sems((64 * deep,)),
            sems((deep,)),
            sems((deep,)),
            sems((4, parts)),
            sems((parts,)),
            sems((blocks,)),
            sems((blocks,)),
            sems((blocks,)),
        ],
        compiler_params=pltpu.CompilerParams(
            collective_id=0, has_side_effects=True, vmem_limit_bytes=VMEM_LIMIT
        ),
        name="whole_step",
    )(
        token_ids.reshape(deep, 2, own_rows).transpose(1, 0, 2).reshape(2, deep * own_rows, 1),
        embed_table,
        w_qkv,
        w_out,
        jnp.stack([ln_gain, ln_bias]),
        centroids_t,
        assignments.reshape(blocks // 2, 1, 2 * own_rows),
    )
    return loss.reshape(own_rows), new


def plan(mesh):
    dp_size, fsdp_size = mesh.shape["dp"], mesh.shape["fsdp"]

    def either(*args):
        few_tokens = args[7].shape[0] <= args[6].shape[1]
        paired = dp_size == 4 and fsdp_size % 2 == 0
        return token_shards(*args) if few_tokens and paired else shards(*args)

    return either


def solution(mesh):
    return jax.shard_map(
        plan(mesh),
        mesh=mesh,
        in_specs=(
            P("dp"),
            P("fsdp", None),
            P("fsdp", None),
            P("fsdp", None),
            P(),
            P(),
            P("fsdp", "dp"),
            P(),
        ),
        out_specs=(P(("dp", "fsdp")), P(("dp", "fsdp"), None)),
        check_vma=False,
    )
```

profile of v0, /device:TPU:0, one launch (start us, length us, event | category | flops | bytes accessed | tf_op | source)
XLA Modules:
  0.0 136.8 jit_solution(10549215433164825752)
XLA Ops:
  0.6 0.7 stack.9
  1.3 0.7 stack.10
  2.0 0.6 pad_maximum_fusion.norm_ref
  2.6 1.7 %copy.10.ids_ref = s32[2,512,1]{2,1,0:T(8,128)} copy(s32[2,512,1]{1,0,2:T(2,128)} %bitcast.8) | data formatting | bytes 8192 | tf_op jit(solution)/shard_map/reshape | solution.py:591
  4.3 127.5 %whole_step.1 = (f32[1,128]{1,0:T(1,128)}, f32[1024,768]{1,0:T(8,128)}) custom-call(s32[2,512,1]{2,1,0:T(8,128)} %copy.10.ids_ref, bf16[1908,768]{1,0:T(8,128)(2,1)} %table_ref.1, bf16[96,2304]{1,0:T(8,128)(2,1)} %qkv_ref.1, bf16[96,768]{1,0:T(8,128)(2,1)} %out_w_ref.1, f32[2,768]{1,0:T(2,128)} %pad_maximum_fusion.norm_ref, bf16[96,8192]{1,0:T(8,128)(2,1)} %cent_ref.1, ...), custom_call_target="tpu_custom_call" | custom-call | tf_op jit(solution)/shard_map/whole_step/pallas_call | solution.py:547
  131.8 1.2 copy.13
  133.0 3.8 %copy.14 = f32[1024,768]{1,0:T(8,128)} copy(f32[1024,768]{1,0:T(8,128)} %get-tuple-element.9) | data formatting | bytes 6291456
where the time goes:
time: 139 us; the launch traced here: 137 us
  Pallas kernels  128 us (92%)
  local copies, waits for them, and re-layouts  8.03 us (6%)
    pallas_call x1, Pallas kernels, token_shards(): pl.pallas_call(functools.partial(step_kernel, deep), out_shape=(jax.Shape...  128 us
    unnamed x2, local copies, waits for them, and re-layouts  4.95 us

commit v1 on v0

--- a/solution.py
+++ b/solution.py
@@ -156,7 +156,8 @@
     return (token_loss, new_centroids)
 
 
-VMEM_LIMIT = 60 * 1024 * 1024
+VMEM_LIMIT = 46 * 1024 * 1024
+CUTS = 2
 WHOLE_VMEM = pl.BlockSpec(memory_space=pltpu.VMEM)
 
 
@@ -183,7 +184,8 @@
             there = {"dp": peer // (2 * self.deep), "fsdp": peer % (2 * self.deep)}
             pl.semaphore_signal(barrier, inc=1, device_id=there, device_id_type=pl.DeviceIdType.MESH)
 
-        pl.semaphore_wait(barrier, everyone - 1)
+    def met(self):
+        pl.semaphore_wait(pltpu.get_barrier_semaphore(), 8 * self.deep - 1)
 
 
 class Sender:
@@ -258,31 +260,41 @@
 
 def step_kernel(
     deep,
-    ids_ref,
-    table_ref,
-    qkv_ref,
-    out_w_ref,
-    norm_ref,
-    cent_ref,
-    assign_ref,
+    ids_hbm,
+    table_hbm,
+    qkv_hbm,
+    out_w_hbm,
+    gain_hbm,
+    bias_hbm,
+    cent_hbm,
+    assign_hbm,
     loss_ref,
     new_ref,
+    ids,
+    table,
+    gain,
+    bias,
+    assign,
+    id_columns,
     rows,
     w,
     from_y,
     joined_y,
-    from_z,
+    from_mate,
+    from_far,
     cent,
     old,
     mine,
     tokens,
+    hot,
     counts,
     stat,
     got,
     load_sems,
     send_sems,
     y_sems,
-    z_sems,
+    mate_sems,
+    far_sems,
     w_sems,
     cent_sems,
     token_sems,
@@ -293,108 +305,164 @@
     x, c, z, y = place.x, place.c, place.z, place.y
     own = place.fsdp
     parts = 2 * deep
-    vocab_rows, width = table_ref.shape
+    vocab_rows, width = table.shape
     own_rows = mine.shape[0]
     per_dev = new_ref.shape[0]
     blocks = 4 * parts
-    own_block = place.dp * parts + own
+    own_block = (z * 4 + place.dp) * 2 + y
     quarter, across = x * 2 + c, (1 - x) * 2 + c
     partner, x_side, y_side = place.at(c=1 - c), place.at(x=1 - x), place.at(y=1 - y)
     up, down = place.at(z=jnp.minimum(z + 1, deep - 1)), place.at(z=jnp.maximum(z - 1, 0))
-
-    loads = []
+    outer = (z == 0) | (z == 3)
+    inner = (z == 1) | (z == 2)
+    mate_z = z + 1 - 2 * (z % 2)
+    mate = place.at(z=mate_z)
+    far = [3 - 3 * (z // 2), 2 - z // 2]
+    dests = far + [mate_z, z]
+
+    loads = [
+        pltpu.make_async_copy(ids_hbm, ids, load_sems.at[0]),
+        pltpu.make_async_copy(table_hbm, table, load_sems.at[1]),
+    ]
     for q in range(4):
-        part = qkv_ref.at[:, pl.ds(q * width, width)] if q < 3 else out_w_ref
-        loads.append(pltpu.make_async_copy(part, w.at[q, own], load_sems.at[q]))
+        part = qkv_hbm.at[:, pl.ds(q * width, width)] if q < 3 else out_w_hbm
+        loads.append(pltpu.make_async_copy(part, w.at[q, own], load_sems.at[2 + q]))
+    loads.append(pltpu.make_async_copy(gain_hbm, gain, load_sems.at[6]))
+    loads.append(pltpu.make_async_copy(bias_hbm, bias, load_sems.at[7]))
+    loads.append(pltpu.make_async_copy(assign_hbm, assign, load_sems.at[8]))
     loads.append(
         pltpu.make_async_copy(
-            cent_ref.at[:, pl.ds(pl.multiple_of(own * per_dev, 128), per_dev)], cent.at[own], load_sems.at[4]
+            cent_hbm.at[:, pl.ds(pl.multiple_of(own * per_dev, 128), per_dev)], cent.at[own], load_sems.at[9]
         )
     )
     for load in loads:
         load.start()
+    place.greet()
+    loads[0].wait()
+    columns = ids[...].T
+    for k in range(parts):
+        id_columns[k // 2, k % 2] = columns[:, k : k + 1]
+    loads[1].wait()
 
     def look(y0):
-        local = ids_ref[y0] - own * vocab_rows
+        local = id_columns[:, y0].reshape(deep * own_rows, 1) - own * vocab_rows
         hot = local == lax.broadcasted_iota(jnp.int32, (deep * own_rows, vocab_rows), 1)
         found = jnp.dot(
-            jnp.where(hot, 1.0, 0.0).astype(jnp.bfloat16), table_ref[...], preferred_element_type=jnp.float32
+            jnp.where(hot, 1.0, 0.0).astype(jnp.bfloat16), table[...], preferred_element_type=jnp.float32
         )
         rows[y0] = found.astype(jnp.bfloat16).reshape(deep, own_rows, width)
 
-    place.greet()
+    base = (place.dp * parts + own) * per_dev
+    centroid = lax.broadcasted_iota(jnp.int32, (per_dev, 2 * own_rows), 0) + base
+
+    def prepare(z1):
+        @pl.loop(0, 4)
+        def each(i):
+            ones = jnp.where(centroid == assign[i * deep + z1], 1.0, 0.0)
+            hot[z1, :, pl.ds(pl.multiple_of(i * 2 * own_rows, 128), 2 * own_rows)] = ones.astype(jnp.bfloat16)
+            counts[...] += jnp.sum(ones, axis=1, keepdims=True)
+
+    counts[...] = jnp.zeros_like(counts)
+    look(1 - y)
+    for load in loads[2:]:
+        load.wait()
+    place.met()
     out = Sender(send_sems)
-    for load in loads:
-        load.wait()
-
-    home = w.at[quarter, own]
-    out.send(home, home, w_sems.at[quarter, own], up, z + 1 < deep)
-    out.send(home, home, w_sems.at[quarter, own], down, z > 0)
-    for k in range(1, deep + 1):
-        to = (z + k) % deep
-        if k == 1:
-            look(1 - y)
+
+    def send_rows(to):
         out.send(rows.at[1 - y, to], from_y.at[to], y_sems.at[to], y_side)
+
+    def w_send(q, s, peer, when=None):
+        out.send(w.at[q, s], w.at[q, s], w_sems.at[q, s], peer, when)
+
+    def w_wait(q, s):
+        out.arrived(w.at[q, s], w_sems.at[q, s], partner)
+
+    def give(z0, y0, when=None):
+        to = z0 * 2 + y0
+        part = pl.ds(pl.multiple_of(to * per_dev, 128), per_dev)
+        out.send(
+            cent_hbm.at[:, part], cent.at[own], cent_sems.at[own], {"dp": place.dp, "fsdp": to}, when
+        )
+
+    w_send(quarter, own, up, z + 1 < deep)
+    w_send(quarter, own, down, z > 0)
+    send_rows(dests[0])
+    send_rows(dests[1])
+    w_send(quarter, own, y_side)
+    send_rows(dests[2])
+    send_rows(dests[3])
+    give(mate_z, y)
+    give(3 - z, y, inner)
     look(y)
-
-    def spread(s):
-        block = w.at[quarter, s]
-        out.send(block, block, w_sems.at[quarter, s], x_side)
-        out.send(block, block, w_sems.at[quarter, s], partner)
-
-    def join(k):
-        to = (z + k) % deep
+    prepare(0)
+
+    def w_column(k):
+        z0 = near_first(z, k, deep)
+        s = z0 * 2 + y
+        w_wait(quarter, s)
+        w_send(quarter, s, up, (z0 < z) & (z + 1 < deep))
+        w_send(quarter, s, down, (z0 > z) & (z > 0))
+        w_send(quarter, s, y_side)
+        w_send(quarter, s, x_side)
+        w_send(quarter, s, partner)
+
+    def join(to):
         out.arrived(from_y.at[to], y_sems.at[to], y_side)
         joined_y[to] = from_y[to] + rows[y, to]
-        if k < deep:
-            out.send(joined_y.at[to], from_z.at[deep - k], z_sems.at[deep - k], place.at(z=to))
-
-    for k in range(1, deep):
-        z0 = near_first(z, k, deep)
-        s = z0 * 2 + y
-        block = w.at[quarter, s]
-        out.arrived(block, w_sems.at[quarter, s], y_side)
-        out.send(block, block, w_sems.at[quarter, s], up, (z0 < z) & (z + 1 < deep))
-        out.send(block, block, w_sems.at[quarter, s], down, (z0 > z) & (z > 0))
-        spread(s)
-    for k in range(1, deep + 1):
-        join(k)
-    for k in range(deep):
-        block = w.at[quarter, near_first(z, k, deep) * 2 + y]
-        out.send(block, block, w_sems.at[quarter, near_first(z, k, deep) * 2 + y], y_side)
-
-    def give(z0, y0):
-        to = z0 * 2 + y0
-        columns = pl.ds(pl.multiple_of(to * per_dev, 128), per_dev)
-        out.send(
-            cent_ref.at[:, columns], cent.at[own], cent_sems.at[own], {"dp": place.dp, "fsdp": to}
-        )
-
-    for k in range(1, deep):
-        give((z + k) % deep, y)
+
+    def hand(to, when):
+        out.send(joined_y.at[to], from_mate.at[to], mate_sems.at[to], mate, when)
+
+    def mate_arrived(to, when):
+        out.arrived(from_mate.at[to], mate_sems.at[to], mate, when)
+
+    w_column(1)
+    join(dests[0])
+    hand(dests[0], outer)
+    w_column(2)
+    prepare(1)
+    join(dests[1])
+    hand(dests[1], outer)
+
+    def onward(to):
+        mate_arrived(to, inner)
+
+        @pl.when(inner)
+        def add():
+            joined_y[to] = joined_y[to] + from_mate[to]
+
+        out.send(joined_y.at[to], from_far, far_sems.at[0], place.at(z=to), inner)
+
+    onward(dests[0])
+    w_column(3)
+    prepare(2)
+    join(dests[2])
+    hand(dests[2], None)
+    onward(dests[1])
+    give((z + 2) % deep, y)
+    give(3 - z, y, outer)
+    join(dests[3])
+    prepare(3)
     for k in range(deep):
         s = near_first(z, k, deep) * 2 + (1 - y)
-        out.arrived(w.at[quarter, s], w_sems.at[quarter, s], y_side)
-        spread(s)
+        w_wait(quarter, s)
+        w_send(quarter, s, x_side)
+        w_send(quarter, s, partner)
     for k in range(deep):
         give((z + k) % deep, 1 - y)
     others = [near_first(z, k, deep) * 2 + y for k in range(1, deep)]
     others += [near_first(z, k, deep) * 2 + (1 - y) for k in range(deep)]
     for s in others:
-        block = w.at[across, s]
-        out.arrived(block, w_sems.at[across, s], x_side)
-        out.send(block, block, w_sems.at[across, s], partner)
-    total = joined_y[z]
-    for k in range(1, deep):
-        out.arrived(from_z.at[k], z_sems.at[k], y_side)
-        total = total + from_z[k]
+        w_wait(across, s)
+        w_send(across, s, partner)
+    mate_arrived(z, None)
+    out.arrived(from_far, far_sems.at[0], mate)
+    total = joined_y[z] + from_mate[z] + from_far[...]
     for q in (x * 2 + (1 - c), (1 - x) * 2 + (1 - c)):
         for s in others:
-            out.arrived(w.at[q, s], w_sems.at[q, s], partner)
-    for first in range(0, own_rows, SEQ):
-        mine[pl.ds(first, SEQ), :] = passage(
-            total[first : first + SEQ], range(4), norm_ref[0:1, :], norm_ref[1:2, :], w
-        )
+            w_wait(q, s)
+    mine[...] = passage(total, range(4), gain[...], bias[...], w)
 
     x_first = c == 1
     second_xy = (jnp.where(x_first, 1 - x, x), jnp.where(x_first, y, 1 - y))
@@ -403,51 +471,62 @@
     third = place.at(x=third_xy[0], y=third_xy[1])
 
     def number(x0, c0, z0, y0):
-        return ((x0 * 2 + c0) * deep + z0) * 2 + y0
-
-    def push(b, peer, when=None, src=None):
-        block = tokens.at[b]
-        out.send(block if src is None else src, block, token_sems.at[b], peer, when)
-
-    def wait(b):
-        out.arrived(tokens.at[b], token_sems.at[b], partner)
-
-    push(own_block, up, z + 1 < deep, mine)
-    push(own_block, down, z > 0, mine)
-    for peer in (second, third, partner):
-        push(own_block, peer, None, mine)
+        return (z0 * 4 + x0 * 2 + c0) * 2 + y0
+
+    cut_rows = own_rows // CUTS
+
+    def push(b, h, peer, when=None, src=None):
+        lines = pl.ds(h * cut_rows, cut_rows)
+        there = tokens.at[b, lines]
+        out.send(there if src is None else src.at[lines], there, token_sems.at[b, h], peer, when)
+
+    def wait(b, h):
+        out.arrived(tokens.at[b, pl.ds(h * cut_rows, cut_rows)], token_sems.at[b, h], partner)
+
+    for h in range(CUTS):
+        push(own_block, h, up, z + 1 < deep, mine)
+        push(own_block, h, down, z > 0, mine)
+        for peer in (second, third, partner):
+            push(own_block, h, peer, None, mine)
     tokens[own_block] = mine[...]
-    new_ref[...] = jnp.zeros_like(new_ref)
-    counts[...] = jnp.zeros_like(counts)
-    base = own_block * per_dev
-    centroid = lax.broadcasted_iota(jnp.int32, (per_dev, 2 * own_rows), 0) + base
-
-    def pair_of(p):
-        hits = centroid == assign_ref[p]
-        return hits, tokens[pl.ds(p * 2, 2)].reshape(2 * own_rows, width)
-
-    def add_up(p):
-        hits, some = pair_of(p)
-        ones = jnp.where(hits, 1.0, 0.0)
-        counts[...] += jnp.sum(ones, axis=1, keepdims=True)
-        new_ref[...] += jnp.dot(
-            ones.astype(jnp.bfloat16), some, preferred_element_type=jnp.float32
-        )
-
-    def score(p):
-        hits, some = pair_of(p)
+
+    def add_up(k, part, of):
+        z1 = near_first(z, k, deep)
+        span = pl.ds(part * per_dev // of, per_dev // of)
+        term = jnp.dot(
+            hot[z1, span, :],
+            tokens[pl.ds(z1 * 8, 8)].reshape(8 * own_rows, width),
+            preferred_element_type=jnp.float32,
+        )
+        if k == 0:
+            new_ref[span, :] = term
+        else:
+            new_ref[span, :] += term
+
+    def score(z1, i):
+        first = z1 * 8 + i * 2
         logits = lax.dot_general(
-            old[...], some, (((1,), (1,)), ((), ())), preferred_element_type=jnp.float32
+            old[...],
+            tokens[pl.ds(first, 2)].reshape(2 * own_rows, width),
+            (((1,), (1,)), ((), ())),
+            preferred_element_type=jnp.float32,
         )
         peak = jnp.max(logits, axis=0, keepdims=True)
         mass = jnp.sum(jnp.exp(logits - peak), axis=0, keepdims=True)
+        hits = centroid == assign[i * deep + z1]
         pick = jnp.sum(jnp.where(hits, logits, 0.0), axis=0, keepdims=True)
         for half in range(2):
-            b = p * 2 + half
             at = slice(half * own_rows, (half + 1) * own_rows)
             for k, row in enumerate((peak, mass, pick)):
-                stat[b, pl.ds(k, 1), :] = row[:, at]
-            pl.when(b != own_block)(stat_copy(b).start)
+                stat[first + half, pl.ds(k, 1), :] = row[:, at]
+            pl.when(first + half != own_block)(stat_copy(first + half).start)
+
+    def scores(k, part, of):
+        z1 = near_first(z, k, deep)
+
+        @pl.loop(part * 4 // of, (part + 1) * 4 // of)
+        def each(i):
+            score(z1, i)
 
     def stat_copy(b):
         return pltpu.make_async_remote_copy(
@@ -455,7 +534,7 @@
             dst_ref=got.at[own_block],
             send_sem=stat_send.at[b],
             recv_sem=stat_recv.at[own_block],
-            device_id={"dp": b // parts, "fsdp": b % parts},
+            device_id={"dp": b % 8 // 2, "fsdp": b // 8 * 2 + b % 2},
             device_id_type=pl.DeviceIdType.MESH,
         )
 
@@ -465,46 +544,66 @@
             out.arrived(cent.at[s], cent_sems.at[s], partner)
         old[...] = cent[...].reshape(width, per_dev).T
 
-    def finish_line(z1):
+    def onward_z(k):
+        z0 = near_first(z, k, deep)
+        b = number(x, c, z0, y)
+        for h in range(CUTS):
+            wait(b, h)
+            push(b, h, up, (z0 < z) & (z + 1 < deep))
+            push(b, h, down, (z0 > z) & (z > 0))
+            push(b, h, second)
+            push(b, h, third)
+            push(b, h, partner)
+
+    def onward_second(k):
+        b = number(second_xy[0], c, near_first(z, k, deep), second_xy[1])
+        for h in range(CUTS):
+            wait(b, h)
+            push(b, h, third)
+            push(b, h, partner)
+
+    def finish(k):
+        z1 = near_first(z, k, deep)
         for xx, yy in (third_xy, (1 - x, 1 - y)):
             b = number(xx, c, z1, yy)
-            wait(b)
-            push(b, partner)
-
-    def sums_of(z1, with_scores):
+            for h in range(CUTS):
+                wait(b, h)
+                push(b, h, partner)
+
+    def theirs(k):
+        z1 = near_first(z, k, deep)
         for x0 in range(2):
             for y0 in range(2):
-                wait(number(x0, 1 - c, z1, y0))
-
-        @pl.loop(0, 4)
-        def each(i):
-            add_up(i * deep + z1)
-            if with_scores:
-                score(i * deep + z1)
-
-    for k in range(deep):
-        z0 = near_first(z, k, deep)
-        if k > 0:
-            b = number(x, c, z0, y)
-            wait(b)
-            push(b, up, (z0 < z) & (z + 1 < deep))
-            push(b, down, (z0 > z) & (z > 0))
-            push(b, second)
-            push(b, third)
-            push(b, partner)
-        b = number(second_xy[0], c, z0, second_xy[1])
-        wait(b)
-        push(b, third)
-        push(b, partner)
-        if k >= 1:
-            finish_line(near_first(z, k - 1, deep))
-        if k == deep - 2:
-            take_centroids()
-        if k >= 2:
-            sums_of(near_first(z, k - 2, deep), True)
-    finish_line(near_first(z, deep - 1, deep))
-    for k in range(deep - 2, deep):
-        sums_of(near_first(z, k, deep), True)
+                for h in range(CUTS):
+                    wait(number(x0, 1 - c, z1, y0), h)
+
+    take_centroids()
+    onward_second(0)
+    onward_z(1)
+    finish(0)
+    onward_second(1)
+    theirs(0)
+    add_up(0, 0, 1)
+    scores(0, 0, 2)
+    onward_z(2)
+    finish(1)
+    scores(0, 1, 2)
+    onward_second(2)
+    theirs(1)
+    add_up(1, 0, 1)
+    scores(1, 0, 2)
+    onward_z(3)
+    finish(2)
+    scores(1, 1, 2)
+    onward_second(3)
+    theirs(2)
+    add_up(2, 0, 1)
+    scores(2, 0, 2)
+    finish(3)
+    scores(2, 1, 2)
+    theirs(3)
+    add_up(3, 0, 1)
+    scores(3, 0, 1)
 
     many = counts[...]
     new_ref[...] = jnp.where(
@@ -544,42 +643,44 @@
     half = jnp.bfloat16
     block = (own_rows, width)
     sems = pltpu.SemaphoreType.DMA
+    in_hbm = pl.BlockSpec(memory_space=pltpu.HBM)
     loss, new = pl.pallas_call(
         functools.partial(step_kernel, deep),
         out_shape=(
             jax.ShapeDtypeStruct((1, own_rows), jnp.float32),
             jax.ShapeDtypeStruct((per_dev, width), jnp.float32),
         ),
-        in_specs=[
-            WHOLE_VMEM,
-            WHOLE_VMEM,
-            WHOLE_VMEM,
-            WHOLE_VMEM,
-            WHOLE_VMEM,
-            pl.BlockSpec(memory_space=pl.ANY),
-            WHOLE_VMEM,
-        ],
+        in_specs=[in_hbm] * 8,
         out_specs=(WHOLE_VMEM, WHOLE_VMEM),
         scratch_shapes=[
+            pltpu.VMEM((parts, own_rows), jnp.int32),
+            pltpu.VMEM(embed_table.shape, half),
+            pltpu.VMEM((1, width), jnp.float32),
+            pltpu.VMEM((1, width), jnp.float32),
+            pltpu.VMEM((blocks // 2, 1, 2 * own_rows), jnp.int32),
+            pltpu.VMEM((deep, 2, own_rows, 1), jnp.int32),
             pltpu.VMEM((2, deep, *block), half),
             pltpu.VMEM((4, parts, feats, width), half),
             pltpu.VMEM((deep, *block), half),
             pltpu.VMEM((deep, *block), half),
             pltpu.VMEM((deep, *block), half),
+            pltpu.VMEM(block, half),
             pltpu.VMEM((parts, feats, per_dev), half),
             pltpu.VMEM((per_dev, width), half),
             pltpu.VMEM(block, half),
             pltpu.VMEM((blocks, *block), half),
+            pltpu.VMEM((deep, per_dev, 8 * own_rows), half),
             pltpu.VMEM((per_dev, 1), jnp.float32),
             pltpu.VMEM((blocks, 8, own_rows), jnp.float32),
             pltpu.VMEM((blocks, 8, own_rows), jnp.float32),
-            sems((5,)),
+            sems((10,)),
             sems((64 * deep,)),
             sems((deep,)),
             sems((deep,)),
+            sems((1,)),
             sems((4, parts)),
             sems((parts,)),
-            sems((blocks,)),
+            sems((blocks, CUTS)),
             sems((blocks,)),
             sems((blocks,)),
         ],
@@ -588,13 +689,19 @@
         ),
         name="whole_step",
     )(
-        token_ids.reshape(deep, 2, own_rows).transpose(1, 0, 2).reshape(2, deep * own_rows, 1),
-        embed_table,
-        w_qkv,
-        w_out,
-        jnp.stack([ln_gain, ln_bias]),
-        centroids_t,
-        assignments.reshape(blocks // 2, 1, 2 * own_rows),
+        *(
+            pltpu.with_memory_space_constraint(array, pltpu.HBM)
+            for array in (
+                token_ids.reshape(parts, own_rows),
+                embed_table,
+                w_qkv,
+                w_out,
+                ln_gain.reshape(1, width),
+                ln_bias.reshape(1, width),
+                centroids_t,
+                assignments.reshape(blocks // 2, 1, 2 * own_rows),
+            )
+        )
     )
     return loss.reshape(own_rows), new
 
@@ -604,7 +711,7 @@
 
     def either(*args):
         few_tokens = args[7].shape[0] <= args[6].shape[1]
-        paired = dp_size == 4 and fsdp_size % 2 == 0
+        paired = dp_size == 4 and fsdp_size == 8
         return token_shards(*args) if few_tokens and paired else shards(*args)
 
     return either

time: 139 us -> 122 us (0.88)
  Pallas kernels: 128 us -> 116 us
  local copies, waits for them, and re-layouts: 8.03 us -> 4.72 us
    pallas_call x1, Pallas kernels: 128 us -> 116 us  [token_shards(): pl.pallas_call(functools.partial(step_kernel, deep), out_shape=(jax.Shape...]
    unnamed x2, local copies, waits for them, and re-layouts: 4.95 us -> 2.18 us
where the time goes in v1:
time: 122 us; the launch traced here: 121 us
  Pallas kernels  116 us (95%)
  local copies, waits for them, and re-layouts  4.72 us (4%)
    pallas_call x1, Pallas kernels, token_shards(): pl.pallas_call(functools.partial(step_kernel, deep), out_shape=(jax.Shape...  116 us

profile of v1, /device:TPU:0, one launch (start us, length us, event | category | flops | bytes accessed | tf_op | source)
XLA Modules:
  0.0 120.9 jit_solution(12973937252552610200)
XLA Ops:
  0.6 1.3 %reshape.20.gain_hbm = f32[1,768]{1,0:T(1,128)} reshape(f32[768]{0:T(1024)} %param.12) | data formatting | bytes 6144 | tf_op jit(solution)/shard_map/reshape | solution.py:699
  1.9 1.3 %reshape.21.bias_hbm = f32[1,768]{1,0:T(1,128)} reshape(f32[768]{0:T(1024)} %param.13) | data formatting | bytes 6144 | tf_op jit(solution)/shard_map/reshape | solution.py:700
  3.2 115.5 %whole_step.1 = (f32[1,128]{1,0:T(1,128)S(1)}, f32[1024,768]{1,0:T(8,128)S(1)}) custom-call(s32[8,128]{1,0:T(8,128)} %bitcast.5, bf16[1908,768]{1,0:T(8,128)(2,1)} %table_hbm.1, bf16[96,2304]{1,0:T(8,128)(2,1)} %qkv_hbm.1, bf16[96,768]{1,0:T(8,128)(2,1)} %out_w_hbm.1, f32[1,768]{1,0:T(1,128)} %reshape.20.gain_hbm, f32[1,768]{1,0:T(1,128)} %reshape.21.bias_hbm, ...), custom_call_target="tpu_custom_call" | custom-call | tf_op jit(solution)/shard_map/whole_step/pallas_call | solution.py:647
  118.7 0.5 copy.12
  119.2 1.7 %copy.13 = f32[1024,768]{1,0:T(8,128)} copy(f32[1024,768]{1,0:T(8,128)S(1)} %get-tuple-element.9) | data formatting | bytes 6291456

commit v2 on v1

--- a/solution.py
+++ b/solution.py
@@ -275,6 +275,7 @@
     gain,
     bias,
     assign,
+    assign_plane,
     id_columns,
     rows,
     w,
@@ -356,6 +357,9 @@
     centroid = lax.broadcasted_iota(jnp.int32, (per_dev, 2 * own_rows), 0) + base
 
     def prepare(z1):
+        for i in range(4):
+            assign_plane[z1, :, i * 2 * own_rows : (i + 1) * 2 * own_rows] = assign[i * deep + z1]
+
         @pl.loop(0, 4)
         def each(i):
             ones = jnp.where(centroid == assign[i * deep + z1], 1.0, 0.0)
@@ -422,6 +426,7 @@
     hand(dests[0], outer)
     w_column(2)
     prepare(1)
+    give(3 - z, 1 - y)
     join(dests[1])
     hand(dests[1], outer)
 
@@ -449,8 +454,9 @@
         w_wait(quarter, s)
         w_send(quarter, s, x_side)
         w_send(quarter, s, partner)
-    for k in range(deep):
-        give((z + k) % deep, 1 - y)
+    give((z + 2) % deep, 1 - y)
+    give(mate_z, 1 - y)
+    give(z, 1 - y)
     others = [near_first(z, k, deep) * 2 + y for k in range(1, deep)]
     others += [near_first(z, k, deep) * 2 + (1 - y) for k in range(deep)]
     for s in others:
@@ -503,30 +509,43 @@
         else:
             new_ref[span, :] += term
 
-    def score(z1, i):
-        first = z1 * 8 + i * 2
-        logits = lax.dot_general(
-            old[...],
-            tokens[pl.ds(first, 2)].reshape(2 * own_rows, width),
-            (((1,), (1,)), ((), ())),
-            preferred_element_type=jnp.float32,
-        )
-        peak = jnp.max(logits, axis=0, keepdims=True)
-        mass = jnp.sum(jnp.exp(logits - peak), axis=0, keepdims=True)
-        hits = centroid == assign[i * deep + z1]
-        pick = jnp.sum(jnp.where(hits, logits, 0.0), axis=0, keepdims=True)
-        for half in range(2):
-            at = slice(half * own_rows, (half + 1) * own_rows)
-            for k, row in enumerate((peak, mass, pick)):
-                stat[first + half, pl.ds(k, 1), :] = row[:, at]
-            pl.when(first + half != own_block)(stat_copy(first + half).start)
-
-    def scores(k, part, of):
+    def scores(k):
         z1 = near_first(z, k, deep)
-
-        @pl.loop(part * 4 // of, (part + 1) * 4 // of)
-        def each(i):
-            score(z1, i)
+        plane = tokens[pl.ds(z1 * 8, 8)].reshape(8 * own_rows, width)
+        chunk = math.gcd(per_dev, 256)
+        target = assign_plane[z1] - base
+
+        def logits_of(first):
+            return lax.dot_general(
+                old[first : first + chunk, :], plane, (((1,), (1,)), ((), ())), preferred_element_type=jnp.float32
+            )
+
+        line = lax.broadcasted_iota(jnp.int32, (chunk, 8 * own_rows), 0)
+        later = logits_of(0)
+        for first in range(0, per_dev, chunk):
+            logits = later
+            if first + chunk < per_dev:
+                later = logits_of(first + chunk)
+            top = jnp.max(logits, axis=0, keepdims=True)
+            found = jnp.sum(jnp.where(line == target - first, logits, 0.0), axis=0, keepdims=True)
+            if first == 0:
+                peak, pick = top, found
+                mass = jnp.sum(jnp.exp(logits - peak), axis=0, keepdims=True)
+            else:
+                higher = jnp.maximum(peak, top)
+                mass = mass * jnp.exp(peak - higher) + jnp.sum(
+                    jnp.exp(logits - higher), axis=0, keepdims=True
+                )
+                peak, pick = higher, pick + found
+        for i in range(8):
+            at = slice(i * own_rows, (i + 1) * own_rows)
+            for n, row in enumerate((peak, mass, pick)):
+                stat[z1 * 8 + i, pl.ds(n, 1), :] = row[:, at]
+
+        @pl.loop(0, 8)
+        def tell(i):
+            b = z1 * 8 + i
+            pl.when(b != own_block)(stat_copy(b).start)
 
     def stat_copy(b):
         return pltpu.make_async_remote_copy(
@@ -577,33 +596,30 @@
                 for h in range(CUTS):
                     wait(number(x0, 1 - c, z1, y0), h)
 
+    onward_z(1)
+    onward_second(0)
+    onward_z(2)
+    onward_second(1)
+    onward_z(3)
+    finish(0)
+    onward_second(2)
+    finish(1)
+    onward_second(3)
+    theirs(0)
     take_centroids()
-    onward_second(0)
-    onward_z(1)
-    finish(0)
-    onward_second(1)
-    theirs(0)
     add_up(0, 0, 1)
-    scores(0, 0, 2)
-    onward_z(2)
-    finish(1)
-    scores(0, 1, 2)
-    onward_second(2)
+    scores(0)
+    finish(2)
     theirs(1)
     add_up(1, 0, 1)
-    scores(1, 0, 2)
-    onward_z(3)
-    finish(2)
-    scores(1, 1, 2)
-    onward_second(3)
+    scores(1)
+    finish(3)
     theirs(2)
     add_up(2, 0, 1)
-    scores(2, 0, 2)
-    finish(3)
-    scores(2, 1, 2)
+    scores(2)
     theirs(3)
     add_up(3, 0, 1)
-    scores(3, 0, 1)
+    scores(3)
 
     many = counts[...]
     new_ref[...] = jnp.where(
@@ -658,6 +674,7 @@
             pltpu.VMEM((1, width), jnp.float32),
             pltpu.VMEM((1, width), jnp.float32),
             pltpu.VMEM((blocks // 2, 1, 2 * own_rows), jnp.int32),
+            pltpu.VMEM((deep, 1, 8 * own_rows), jnp.int32),
             pltpu.VMEM((deep, 2, own_rows, 1), jnp.int32),
             pltpu.VMEM((2, deep, *block), half),
             pltpu.VMEM((4, parts, feats, width), half),

time: 122 us -> 109 us (0.89); the launches traced: 121 us -> 109 us
  Pallas kernels: 116 us -> 104 us
    pallas_call x1, Pallas kernels: 116 us -> 104 us  [token_shards(): pl.pallas_call(functools.partial(step_kernel, deep), out_shape=(jax.Shape...]
where the time goes in v2:
time: 109 us
  Pallas kernels  104 us (95%)
  local copies, waits for them, and re-layouts  4.72 us (4%)
    pallas_call x1, Pallas kernels, token_shards(): pl.pallas_call(functools.partial(step_kernel, deep), out_shape=(jax.Shape...  104 us

profile of v2, /device:TPU:0, one launch (start us, length us, event | category | flops | bytes accessed | tf_op | source)
XLA Modules:
  0.0 109.1 jit_solution(6588798986729493028)
XLA Ops:
  0.6 1.3 %reshape.20.gain_hbm = f32[1,768]{1,0:T(1,128)} reshape(f32[768]{0:T(1024)} %param.12) | data formatting | bytes 6144 | tf_op jit(solution)/shard_map/reshape | solution.py:716
  1.9 1.3 %reshape.21.bias_hbm = f32[1,768]{1,0:T(1,128)} reshape(f32[768]{0:T(1024)} %param.13) | data formatting | bytes 6144 | tf_op jit(solution)/shard_map/reshape | solution.py:717
  3.2 103.8 %whole_step.1 = (f32[1,128]{1,0:T(1,128)S(1)}, f32[1024,768]{1,0:T(8,128)S(1)}) custom-call(s32[8,128]{1,0:T(8,128)} %bitcast.5, bf16[1908,768]{1,0:T(8,128)(2,1)} %table_hbm.1, bf16[96,2304]{1,0:T(8,128)(2,1)} %qkv_hbm.1, bf16[96,768]{1,0:T(8,128)(2,1)} %out_w_hbm.1, f32[1,768]{1,0:T(1,128)} %reshape.20.gain_hbm, f32[1,768]{1,0:T(1,128)} %reshape.21.bias_hbm, ...), custom_call_target="tpu_custom_call" | custom-call | tf_op jit(solution)/shard_map/whole_step/pallas_call | solution.py:663
  106.9 0.5 copy.12
  107.5 1.7 %copy.13 = f32[1024,768]{1,0:T(8,128)} copy(f32[1024,768]{1,0:T(8,128)S(1)} %get-tuple-element.9) | data formatting | bytes 6291456

commit v3 on v2

--- a/solution.py
+++ b/solution.py
@@ -425,7 +425,6 @@
     join(dests[0])
     hand(dests[0], outer)
     w_column(2)
-    prepare(1)
     give(3 - z, 1 - y)
     join(dests[1])
     hand(dests[1], outer)
@@ -441,14 +440,12 @@
 
     onward(dests[0])
     w_column(3)
-    prepare(2)
     join(dests[2])
     hand(dests[2], None)
     onward(dests[1])
     give((z + 2) % deep, y)
     give(3 - z, y, outer)
     join(dests[3])
-    prepare(3)
     for k in range(deep):
         s = near_first(z, k, deep) * 2 + (1 - y)
         w_wait(quarter, s)
@@ -457,6 +454,8 @@
     give((z + 2) % deep, 1 - y)
     give(mate_z, 1 - y)
     give(z, 1 - y)
+    for k in range(1, deep):
+        prepare(k)
     others = [near_first(z, k, deep) * 2 + y for k in range(1, deep)]
     others += [near_first(z, k, deep) * 2 + (1 - y) for k in range(deep)]
     for s in others:
@@ -551,8 +550,8 @@
         return pltpu.make_async_remote_copy(
             src_ref=stat.at[b],
             dst_ref=got.at[own_block],
-            send_sem=stat_send.at[b],
-            recv_sem=stat_recv.at[own_block],
+            send_sem=stat_send.at[0],
+            recv_sem=stat_recv.at[0],
             device_id={"dp": b % 8 // 2, "fsdp": b // 8 * 2 + b % 2},
             device_id_type=pl.DeviceIdType.MESH,
         )
@@ -615,32 +614,21 @@
     scores(1)
     finish(3)
     theirs(2)
-    add_up(2, 0, 1)
     scores(2)
     theirs(3)
+    scores(3)
+    add_up(2, 0, 1)
     add_up(3, 0, 1)
-    scores(3)
 
     many = counts[...]
     new_ref[...] = jnp.where(
         many > 0, new_ref[...] / jnp.maximum(many, 1.0), old[...].astype(jnp.float32)
     )
-    got[own_block] = stat[own_block]
-
-    @pl.loop(0, blocks)
-    def each_device(b):
-        @pl.when(b != own_block)
-        def done():
-            stat_copy(b).wait_send()
-            pltpu.make_async_remote_copy(
-                src_ref=got.at[b],
-                dst_ref=got.at[b],
-                send_sem=stat_send.at[b],
-                recv_sem=stat_recv.at[b],
-                device_id=partner,
-                device_id_type=pl.DeviceIdType.MESH,
-            ).wait_recv()
-
+    own_stat = pltpu.make_async_copy(stat.at[own_block], got.at[own_block], stat_recv.at[0])
+    own_stat.start()
+    sent = stat.at[pl.ds(0, blocks - 1)]
+    pltpu.make_async_copy(sent, sent, stat_send.at[0]).wait()
+    pltpu.make_async_copy(got, got, stat_recv.at[0]).wait()
     peaks, masses, picks = (got[:, k, :] for k in range(3))
     top = jnp.max(peaks, axis=0, keepdims=True)
     mass = jnp.sum(masses * jnp.exp(peaks - top), axis=0, keepdims=True)
@@ -698,8 +686,8 @@
             sems((4, parts)),
             sems((parts,)),
             sems((blocks, CUTS)),
-            sems((blocks,)),
-            sems((blocks,)),
+            sems((1,)),
+            sems((1,)),
         ],
         compiler_params=pltpu.CompilerParams(
             collective_id=0, has_side_effects=True, vmem_limit_bytes=VMEM_LIMIT

time: 109 us -> 105 us (0.963)
  Pallas kernels: 104 us -> 99.8 us
    pallas_call x1, Pallas kernels: 104 us -> 99.8 us  [token_shards(): pl.pallas_call(functools.partial(step_kernel, deep), out_shape=(jax.Shape...]
where the time goes in v3:
time: 105 us
  Pallas kernels  99.8 us (95%)
  local copies, waits for them, and re-layouts  4.72 us (4%)
    pallas_call x1, Pallas kernels, token_shards(): pl.pallas_call(functools.partial(step_kernel, deep), out_shape=(jax.Shape...  99.8 us
    unnamed x2, local copies, waits for them, and re-layouts  2.18 us

profile of v3, /device:TPU:0, one launch (start us, length us, event | category | flops | bytes accessed | tf_op | source)
XLA Modules:
  0.0 105.1 jit_solution(228116180919794698)
XLA Ops:
  0.6 1.3 %reshape.20.gain_hbm = f32[1,768]{1,0:T(1,128)} reshape(f32[768]{0:T(1024)} %param.12) | data formatting | bytes 6144 | tf_op jit(solution)/shard_map/reshape | solution.py:704
  1.9 1.3 %reshape.21.bias_hbm = f32[1,768]{1,0:T(1,128)} reshape(f32[768]{0:T(1024)} %param.13) | data formatting | bytes 6144 | tf_op jit(solution)/shard_map/reshape | solution.py:705
  3.2 99.8 %whole_step.1 = (f32[1,128]{1,0:T(1,128)S(1)}, f32[1024,768]{1,0:T(8,128)S(1)}) custom-call(s32[8,128]{1,0:T(8,128)} %bitcast.5, bf16[1908,768]{1,0:T(8,128)(2,1)} %table_hbm.1, bf16[96,2304]{1,0:T(8,128)(2,1)} %qkv_hbm.1, bf16[96,768]{1,0:T(8,128)(2,1)} %out_w_hbm.1, f32[1,768]{1,0:T(1,128)} %reshape.20.gain_hbm, f32[1,768]{1,0:T(1,128)} %reshape.21.bias_hbm, ...), custom_call_target="tpu_custom_call" | custom-call | tf_op jit(solution)/shard_map/whole_step/pallas_call | solution.py:651
  103.0 0.5 copy.12
  103.5 1.7 %copy.13 = f32[1024,768]{1,0:T(8,128)} copy(f32[1024,768]{1,0:T(8,128)S(1)} %get-tuple-element.9) | data formatting | bytes 6291456

commit v4 on v3

--- a/solution.py
+++ b/solution.py
@@ -399,7 +399,6 @@
     give(mate_z, y)
     give(3 - z, y, inner)
     look(y)
-    prepare(0)
 
     def w_column(k):
         z0 = near_first(z, k, deep)
@@ -454,7 +453,7 @@
     give((z + 2) % deep, 1 - y)
     give(mate_z, 1 - y)
     give(z, 1 - y)
-    for k in range(1, deep):
+    for k in range(deep):
         prepare(k)
     others = [near_first(z, k, deep) * 2 + y for k in range(1, deep)]
     others += [near_first(z, k, deep) * 2 + (1 - y) for k in range(deep)]

time: 105 us -> 105 us (level)
  no operation moved by 1% of the time
where the time goes in v4:
time: 105 us
  Pallas kernels  99.8 us (95%)
  local copies, waits for them, and re-layouts  4.72 us (4%)
    pallas_call x1, Pallas kernels, token_shards(): pl.pallas_call(functools.partial(step_kernel, deep), out_shape=(jax.Shape...  99.8 us
    unnamed x2, local copies, waits for them, and re-layouts  2.18 us

profile of v4, /device:TPU:0, one launch (start us, length us, event | category | flops | bytes accessed | tf_op | source)
XLA Modules:
  0.0 105.1 jit_solution(5391117624713538805)
XLA Ops:
  0.6 1.3 %reshape.20.gain_hbm = f32[1,768]{1,0:T(1,128)} reshape(f32[768]{0:T(1024)} %param.12) | data formatting | bytes 6144 | tf_op jit(solution)/shard_map/reshape | solution.py:703
  1.9 1.3 %reshape.21.bias_hbm = f32[1,768]{1,0:T(1,128)} reshape(f32[768]{0:T(1024)} %param.13) | data formatting | bytes 6144 | tf_op jit(solution)/shard_map/reshape | solution.py:704
  3.2 99.8 %whole_step.1 = (f32[1,128]{1,0:T(1,128)S(1)}, f32[1024,768]{1,0:T(8,128)S(1)}) custom-call(s32[8,128]{1,0:T(8,128)} %bitcast.5, bf16[1908,768]{1,0:T(8,128)(2,1)} %table_hbm.1, bf16[96,2304]{1,0:T(8,128)(2,1)} %qkv_hbm.1, bf16[96,768]{1,0:T(8,128)(2,1)} %out_w_hbm.1, f32[1,768]{1,0:T(1,128)} %reshape.20.gain_hbm, f32[1,768]{1,0:T(1,128)} %reshape.21.bias_hbm, ...), custom_call_target="tpu_custom_call" | custom-call | tf_op jit(solution)/shard_map/whole_step/pallas_call | solution.py:650
  102.9 0.5 copy.12
  103.5 1.7 %copy.13 = f32[1024,768]{1,0:T(8,128)} copy(f32[1024,768]{1,0:T(8,128)S(1)} %get-tuple-element.9) | data formatting | bytes 6291456
